TPU v7x, 32 devices: a whole 2x2x4 slice. The times are simulated.
32 devices in a mesh: dom: 8 (over z, y), rows: 4 (over x, core).
Axes of the slice: x: 2, y: 2, z: 4, core: 2. Of those that a mesh axis runs over, the one named last changes fastest.
Arguments:
- fields: float32 [8, 3, 128, 4096], P('dom', None, 'rows'), may hold values from -6 to 6
- depth: float32 [128, 4096], P('rows'), may hold values from 1.5 to 6
- obs_index: int32 [256], replicated, may hold values from 0 to 524287, as said below
- obs_value: float32 [256], replicated, may hold values from -6 to 6
- obs_var: float32 [256], replicated, may hold values from 0.5 to 5
- parent_lookup: int32 [8], replicated, may hold values from 0 to 7, as said below
Outputs:
- log_weights: float32 [8], P('dom')
- posterior_members: float32 [8, 3, 128, 4096], P('dom', None, 'rows')
Inputs may be any that keep to these rules, and one draw needn't show every extreme that they name: `parent_lookup`: every value is the index of a particle; 0 and 7 each appear; values may repeat. `obs_index`: indices of grid cells, possibly repeated; the first and last cell each appear.
All inputs are finite; a program needn't handle non-finite values.
Results may differ from a plain program's by a relative error of at most 0.00003.
Values sent between devices are 32-bit elements; how exact they have to be, the bound alone decides.
No kernel may reach another device: no remote copies, remote signals or barrier semaphores. Data moves between devices by JAX's collectives and lax.ppermute only.
A program may use at most 64 MiB of HBM per device.

v0:
```python
import jax
import jax.numpy as jnp
from jax import lax
from jax.experimental import pallas as pl
from jax.experimental.pallas import tpu as pltpu
from jax.sharding import PartitionSpec as P

STEPS = 4
HALO = 2 * STEPS
LANES = 128
VMEM_BYTES = 48 * 2**20

time_step = 0.5
coriolis = 0.2

in_vmem = pl.BlockSpec(memory_space=pltpu.VMEM)
in_smem = pl.BlockSpec(memory_space=pltpu.SMEM)
in_hbm = pl.BlockSpec(memory_space=pltpu.HBM)


def forecast_steps(h, u, v, d, top_open=None, bottom_open=None):
    n_rows, n_cols = h.shape
    for _ in range(STEPS):
        du = d * u
        dv = d * v
        dx = 0.5 * (pltpu.roll(du, n_cols - 1, 1) - pltpu.roll(du, 1, 1))
        dy = 0.5 * (pltpu.roll(dv, n_rows - 1, 0) - pltpu.roll(dv, 1, 0))
        h = h - time_step * (dx + dy)
        if top_open is not None:
            h = jnp.concatenate(
                [h[:HALO] * top_open, h[HALO : n_rows - HALO], h[n_rows - HALO :] * bottom_open], axis=0
            )
        dx = 0.5 * (pltpu.roll(h, n_cols - 1, 1) - pltpu.roll(h, 1, 1))
        u = u - time_step * dx + (time_step * coriolis) * v
        dy = 0.5 * (pltpu.roll(h, n_rows - 1, 0) - pltpu.roll(h, 1, 0))
        v = v - time_step * dy - (time_step * coriolis) * u
    return h, u, v


def chunk_width(n_cols, piece):
    return min(512, piece)


def window_columns(rows_of, start, width, n_cols, n_rows):
    left = pl.multiple_of(lax.rem(start + n_cols - LANES, n_cols), LANES)
    right = pl.multiple_of(lax.rem(start + width, n_cols), LANES)
    lane = lax.broadcasted_iota(jnp.int32, (n_rows, LANES), 1)

    def window(k):
        rim = jnp.where(lane < LANES // 2, rows_of(k, right, LANES), rows_of(k, left, LANES))
        return jnp.concatenate([rows_of(k, start, width), rim], axis=1)

    return [window(k) for k in range(4)]


def over_pieces(at_ref, n_cols, outs, work):
    piece = n_cols // len(outs)
    width = chunk_width(n_cols, piece)
    parts = piece // width

    def part(i, carry):
        m = i // parts
        inner = pl.multiple_of(i % parts * width, LANES)
        start = pl.multiple_of(jnp.bitwise_xor(at_ref[0], m) * piece + inner, LANES)
        done = work(start, width)
        for to, out in enumerate(outs):

            @pl.when(m == to)
            def _(out=out):
                for k in range(3):
                    out[k, :, pl.ds(inner, width)] = done[k]

        return carry

    lax.fori_loop(0, len(outs) * parts, part, 0)


def inner_kernel(at_ref, fields_ref, depth_ref, *refs):
    outs, (h_ref, head_ref, tail_ref) = refs[:-3], refs[-3:]
    n_rows, n_cols = depth_ref.shape

    def rows_of(k, at, size):
        return depth_ref[:, pl.ds(at, size)] if k == 3 else fields_ref[0, k, :, pl.ds(at, size)]

    def work(start, width):
        columns = window_columns(rows_of, start, width, n_cols, n_rows)
        for k in range(4):
            head_ref[k, :, pl.ds(start, width)] = columns[k][:HALO, :width]
            tail_ref[k, :, pl.ds(start, width)] = columns[k][n_rows - HALO :, :width]
        done = forecast_steps(*columns)
        done = [x[HALO : n_rows - HALO, :width] for x in done]
        h_ref[:, pl.ds(start, width)] = done[0]
        return done

    over_pieces(at_ref, n_cols, outs, work)


def outer_kernel(at_ref, fields_ref, depth_ref, above_ref, below_ref, *refs):
    outs, h_ref = refs[:-1], refs[-1]
    n_rows, n_cols = depth_ref.shape
    top_open = at_ref[1].astype(jnp.float32)
    bottom_open = at_ref[2].astype(jnp.float32)

    def rows_of(k, at, size):
        mid = depth_ref[:, pl.ds(at, size)] if k == 3 else fields_ref[0, k, :, pl.ds(at, size)]
        return jnp.concatenate([above_ref[k, :, pl.ds(at, size)], mid, below_ref[k, :, pl.ds(at, size)]], axis=0)

    def work(start, width):
        columns = window_columns(rows_of, start, width, n_cols, n_rows + 2 * HALO)
        done = forecast_steps(*columns, top_open, bottom_open)
        done = [jnp.concatenate([x[HALO : 2 * HALO, :width], x[n_rows : n_rows + HALO, :width]], axis=0) for x in done]
        h_ref[:, pl.ds(start, width)] = done[0]
        return done

    over_pieces(at_ref, n_cols, outs, work)


def forecast(kernel, name, at, arrays, n_rows, n_cols, count, extra=()):
    shapes = [(3, n_rows, n_cols // count)] * count + [(n_rows, n_cols)] + list(extra)
    outs = pl.pallas_call(
        kernel,
        out_shape=[jax.ShapeDtypeStruct(shape, jnp.float32) for shape in shapes],
        in_specs=[in_smem] + [in_vmem] * len(arrays),
        out_specs=[in_vmem] * len(shapes),
        compiler_params=pltpu.CompilerParams(vmem_limit_bytes=VMEM_BYTES),
        name=name,
    )(at, *arrays)
    return list(outs[:count]), outs[count:]


def misfit_kernel(at_ref, index_ref, value_ref, var_ref, inner_ref, outer_ref, out_ref, total_ref):
    inner_rows, n_cols = inner_ref.shape
    n_rows = inner_rows + 2 * HALO
    base = at_ref[3] * (n_rows * n_cols)
    row_in = lax.broadcasted_iota(jnp.int32, (8, LANES), 0)
    lane_in = lax.broadcasted_iota(jnp.int32, (8, LANES), 1)

    def tile(ref, row, col):
        first_row = pl.multiple_of(jnp.bitwise_and(row, -8), 8)
        first_col = pl.multiple_of(jnp.bitwise_and(col, -LANES), LANES)
        return ref[pl.ds(first_row, 8), pl.ds(first_col, LANES)]

    def point(k, carry):
        offset = index_ref[k] - base

        @pl.when(jnp.logical_and(offset >= 0, offset < n_rows * n_cols))
        def _():
            row = lax.div(offset, n_cols)
            col = offset - row * n_cols
            inner_row = row - HALO
            is_inner = jnp.logical_and(inner_row >= 0, inner_row < inner_rows)
            outer_row = jnp.where(row < HALO, row, row - inner_rows)
            hit = (row_in == jnp.bitwise_and(row, 7)) & (lane_in == jnp.bitwise_and(col, LANES - 1))

            def add(seen):
                total_ref[...] += jnp.where(hit, (value_ref[k] - seen) ** 2 / var_ref[k], 0.0)

            @pl.when(is_inner)
            def _():
                add(tile(inner_ref, inner_row, col))

            @pl.when(jnp.logical_not(is_inner))
            def _():
                add(tile(outer_ref, outer_row, col))

        return carry

    total_ref[...] = jnp.zeros_like(total_ref)
    lax.fori_loop(0, index_ref.shape[0], point, 0)
    out_ref[...] = jnp.broadcast_to(jnp.sum(total_ref[...]), out_ref.shape)


def misfit(at, obs_index, obs_value, obs_var, inner, outer):
    return pl.pallas_call(
        misfit_kernel,
        out_shape=jax.ShapeDtypeStruct((8, LANES), jnp.float32),
        in_specs=[in_smem] * 4 + [in_vmem] * 2,
        out_specs=in_vmem,
        scratch_shapes=[pltpu.VMEM((8, LANES), jnp.float32)],
        compiler_params=pltpu.CompilerParams(vmem_limit_bytes=VMEM_BYTES),
        name="misfit",
    )(at, obs_index, obs_value, obs_var, inner, outer)[0, 0]


def sum_over(x, axis):
    count = lax.axis_size(axis)
    step = 1
    while step < count:
        x = x + lax.ppermute(x, axis, [(i, i ^ step) for i in range(count)])
        step *= 2
    return x


def log_weight(misfit_sum):
    loglik = sum_over(-0.5 * misfit_sum, "rows")
    slots = lax.broadcasted_iota(jnp.int32, (lax.axis_size("dom"),), 0)
    every = sum_over(jnp.where(slots == lax.axis_index("dom"), loglik, 0.0), "dom")
    peak = jnp.max(every)
    total = jnp.sum(jnp.exp(every - peak))
    return (loglik - (peak + jnp.log(total)))[None]


def place(at, pieces, spans, shape, into=None):
    count = len(pieces)
    n_cols = shape[-1]
    width = n_cols // count

    def kernel(at_ref, *refs):
        srcs = refs[:count]
        dst, sems = refs[-2], refs[-1]
        copies = []
        for m in range(count):
            first = pl.multiple_of(jnp.bitwise_xor(at_ref[0], m) * width, LANES)
            for s, (src_row, dst_row, size) in enumerate(spans):
                copies.append(
                    pltpu.make_async_copy(
                        srcs[m].at[:, pl.ds(src_row, size), :],
                        dst.at[0, :, pl.ds(dst_row, size), pl.ds(first, width)],
                        sems.at[m * len(spans) + s],
                    )
                )
        for c in copies:
            c.start()
        for c in copies:
            c.wait()

    extra = [] if into is None else [into]
    return pl.pallas_call(
        kernel,
        out_shape=pltpu.HBM(shape, jnp.float32),
        in_specs=[in_smem] + [in_vmem] * count + [in_hbm] * len(extra),
        out_specs=in_hbm,
        scratch_shapes=[pltpu.SemaphoreType.DMA((count * len(spans),))],
        input_output_aliases={} if into is None else {count + 1: 0},
        compiler_params=pltpu.CompilerParams(vmem_limit_bytes=VMEM_BYTES),
        name="place",
    )(at, *pieces, *extra)


def route_kernel(at_ref, parents_ref, out_ref, *, half):
    own = at_ref[0]
    side = at_ref[4]
    parents = [parents_ref[s] for s in range(2 * half)]

    def ranks(first):
        other = half - first
        running = jnp.int32(0)
        needed, rank = [], []
        for q in range(half):
            hit = jnp.int32(0)
            for s in range(half):
                hit = hit | jnp.where(parents[other + s] == first + q, 1, 0).astype(jnp.int32)
            needed.append(hit)
            rank.append(running)
            running = running + hit
        return needed, rank, running

    low = ranks(0)
    high = ranks(half)
    out_ref[0] = jnp.maximum(low[2], high[2])
    mine = [jnp.where(side == 0, a, b) for a, b in zip(low[0], high[0])]
    my_rank = [jnp.where(side == 0, a, b) for a, b in zip(low[1], high[1])]
    other_rank = [jnp.where(side == 0, b, a) for a, b in zip(low[1], high[1])]
    for k in range(half):
        chosen = jnp.int32(0)
        for q in range(half):
            chosen = jnp.where((mine[q] == 1) & (my_rank[q] == k), q, chosen)
        out_ref[1 + k] = jnp.bitwise_xor(chosen, own)
    for m in range(half):
        slot = jnp.bitwise_xor(own, m)
        parent = jnp.int32(0)
        for s in range(half):
            parent = jnp.where(slot == s, jnp.where(side == 0, parents[s], parents[half + s]), parent)
        local = parent - side * half
        remote = parent - (1 - side) * half
        from_rank = jnp.int32(0)
        for q in range(half):
            from_rank = jnp.where(remote == q, other_rank[q], from_rank)
        is_local = jnp.logical_and(local >= 0, local < half)
        out_ref[1 + half + m] = jnp.where(is_local, jnp.bitwise_xor(local, own), half + from_rank)


def route(at, parent_lookup, half):
    return pl.pallas_call(
        lambda *refs: route_kernel(*refs, half=half),
        out_shape=jax.ShapeDtypeStruct((1 + 2 * half,), jnp.int32),
        in_specs=[in_smem, in_smem],
        out_specs=in_smem,
        name="route",
    )(at, parent_lookup)


def to_mate(x, m):
    return lax.ppermute(x, "dom", [(i, i ^ m) for i in range(lax.axis_size("dom"))])


def among_mates(pieces):
    return [x if m == 0 else to_mate(x, m) for m, x in enumerate(pieces)]


def chosen(held, routes, crossing):
    return [lax.select_n(routes[1 + k], *held) for k in range(crossing)]


def across(pieces, half):
    return [to_mate(x, half) for x in pieces]


def for_slots(held, got, routes):
    half = len(held)
    return [lax.select_n(routes[1 + half + m], *held, *got) for m in range(half)]


def after(x, *earlier):
    return lax.optimization_barrier((x, earlier))[0]


def halo_rows(head, tail):
    count = lax.axis_size("rows")
    above = lax.ppermute(tail, "rows", [(i, i + 1) for i in range(count - 1)])
    below = lax.ppermute(head, "rows", [(i + 1, i) for i in range(count - 1)])
    return above, below


def inner_forecast(at, fields, depth, count):
    n_rows, n_cols = depth.shape
    rim = (4, HALO, n_cols)
    return forecast(inner_kernel, "inner", at, (fields, depth), n_rows - 2 * HALO, n_cols, count, (rim, rim))


def outer_forecast(at, fields, depth, above, below, count):
    return forecast(outer_kernel, "outer", at, (fields, depth, above, below), 2 * HALO, depth.shape[1], count)


def cycle(crossing, routes, at, fields, depth, obs_index, obs_value, obs_var):
    half = lax.axis_size("dom") // 2
    n_rows, n_cols = depth.shape
    inner, (inner_h, head, tail) = inner_forecast(at, fields, depth, half)
    inner_held = among_mates(inner)
    above, below = halo_rows(head, tail)
    inner_chosen = chosen(inner_held, routes, crossing)
    inner_got = across(inner_chosen, half)
    outer, (outer_h,) = outer_forecast(at, fields, depth, above, after(below, inner_chosen), half)
    outer_held = among_mates(outer)
    outer_chosen = chosen(outer_held, routes, crossing)
    outer_got = across(outer_chosen, half)
    log_weights = log_weight(misfit(at, obs_index, obs_value, obs_var, inner_h, after(outer_h, outer_chosen)))
    inner_done = among_mates(for_slots(inner_held, after(inner_got, outer), routes))
    outer_done = among_mates(for_slots(outer_held, outer_got, routes))
    members = place(at, inner_done, ((0, HALO, n_rows - 2 * HALO),), fields.shape)
    members = place(at, outer_done, ((0, 0, HALO), (HALO, n_rows - HALO, HALO)), fields.shape, members)
    return log_weights, members


def shards(fields, depth, obs_index, obs_value, obs_var, parent_lookup):
    rows_at = lax.axis_index("rows")
    dom_at = lax.axis_index("dom")
    half = lax.axis_size("dom") // 2
    at = jnp.stack(
        [dom_at % half, rows_at > 0, rows_at < lax.axis_size("rows") - 1, rows_at, dom_at // half]
    ).astype(jnp.int32)
    if half == 4:
        routes = route(at, parent_lookup, half)
        branches = [
            (lambda r, a, *rest, c=c: cycle(c, r, a, *rest)) for c in range(1, half + 1)
        ]
        return lax.switch(
            jnp.clip(routes[0] - 1, 0, half - 1), branches, routes, at, fields, depth, obs_index, obs_value, obs_var
        )
    return by_pieces(at, fields, depth, obs_index, obs_value, obs_var, parent_lookup)


def by_pieces(at, fields, depth, obs_index, obs_value, obs_var, parent_lookup):
    pieces = lax.axis_size("dom")
    n_rows, n_cols = depth.shape
    whole = at * jnp.array([0, 1, 1, 1, 1], jnp.int32)
    (inner,), (inner_h, head, tail) = inner_forecast(whole, fields, depth, 1)
    (outer,), (outer_h,) = outer_forecast(whole, fields, depth, *halo_rows(head, tail), 1)
    log_weights = log_weight(misfit(at, obs_index, obs_value, obs_var, inner_h, outer_h))
    slab = jnp.concatenate([outer[:, :HALO], inner, outer[:, HALO:]], axis=1)
    tiles = slab.reshape(3, n_rows, pieces, n_cols // pieces).transpose(2, 0, 1, 3)
    received = lax.all_to_all(tiles, "dom", split_axis=0, concat_axis=0, tiled=True)
    picked = jnp.take(received, parent_lookup, axis=0, mode="clip")
    final = lax.all_to_all(picked, "dom", split_axis=0, concat_axis=0, tiled=True)
    return log_weights, final.transpose(1, 2, 0, 3).reshape(1, 3, n_rows, n_cols)


def solution(mesh):
    in_specs = (P("dom", None, "rows", None), P("rows", None), P(), P(), P(), P())
    out_specs = (P("dom"), P("dom", None, "rows", None))
    return jax.shard_map(shards, mesh=mesh, in_specs=in_specs, out_specs=out_specs, check_vma=False)
```

profile of v0, /device:TPU:0, one launch (start us, length us, event | category | flops | bytes accessed | tf_op | source)
XLA Modules:
  0.0 108.7 jit_solution(14601288315626627803)
XLA Ops:
  2.1 105.5 %conditional.1 = (f32[1]{0:T(128)}, f32[1,3,32,4096]{3,2,1,0:T(8,128)}) conditional(s32[]{:T(128)} %bitcast.131, (s32[5]{0:T(128)S(1)}, f32[1,3,32,4096]{3,2,1,0:T(8,128)}, f32[32,4096]{1,0:T(8,128)}, s32[9]{0:T(128)S(1)}, s32[256]{0:T(256)}, /*index=5*/f32[256]{0:T(256)}, f32[256]{0:T(256)}) %tuple.35, ...), branch_computations={%region_0.3_spmd, %region_3.6_spmd, %region_6.9_spmd, %region_9.12... | conditional | flops 3932310 | bytes 39336472 | solution.py:367
  2.2 8.0 %inner.5 = (f32[3,16,1024]{2,1,0:T(8,128)S(1)}, f32[3,16,1024]{2,1,0:T(8,128)S(1)}, f32[3,16,1024]{2,1,0:T(8,128)S(1)}, f32[3,16,1024]{2,1,0:T(8,128)S(1)}, f32[...) custom-call(s32[5]{0:T(128)S(1)} %get-tuple-element.78.at_ref, ...), custom_call_target="tpu_custom_call" | custom-call | tf_op jit(solution)/shard_map/cond/branch_1_fun/inner/pallas_call | solution.py:120
  10.1 3.0 %collective-permute-start.23 = (f32[3,16,1024]{2,1,0:T(8,128)S(1)}, f32[3,16,1024]{2,1,0:T(8,128)S(1)}, u32[]{:S(2)}, u32[]{:S(2)}) collective-permute-start(f32[3,16,1024]{2,1,0:T(8,128)S(1)} %get-tuple-element.89), channel_id=1, source_target_pairs={{0,4},{4,0},{8,12},{12,8},{16,20},{20,16},{24,28},{28,24},{1,5},{5... | collective-permute-start | bytes 589832 | tf_op jit(solution)/shard_map/cond/branch_1_fun/ppermute | solution.py:294
  13.2 1.6 %collective-permute-start.24 = (f32[3,16,1024]{2,1,0:T(8,128)S(1)}, f32[3,16,1024]{2,1,0:T(8,128)S(1)}, u32[]{:S(2)}, u32[]{:S(2)}) collective-permute-start(f32[3,16,1024]{2,1,0:T(8,128)S(1)} %get-tuple-element.90), channel_id=1, source_target_pairs={{0,8},{4,12},{8,0},{12,4},{16,24},{20,28},{24,16},{28,20},{1,9},{5... | collective-permute-start | bytes 589832 | tf_op jit(solution)/shard_map/cond/branch_1_fun/ppermute | solution.py:294
  21.9 1.6 %collective-permute-done.25 = f32[3,16,1024]{2,1,0:T(8,128)S(1)} collective-permute-done((f32[3,16,1024]{2,1,0:T(8,128)S(1)}, f32[3,16,1024]{2,1,0:T(8,128)S(1)}, u32[]{:S(2)}, u32[]{:S(2)}) %collective-permute-start.25) | collective-permute-done | bytes 196640 | tf_op jit(solution)/shard_map/cond/branch_1_fun/ppermute | solution.py:294
  25.0 2.7 %collective-permute-start.40 = (f32[3,16,1024]{2,1,0:T(8,128)}, f32[3,16,1024]{2,1,0:T(8,128)}, u32[]{:S(2)}, u32[]{:S(2)}) collective-permute-start(f32[3,16,1024]{2,1,0:T(8,128)} %get-tuple-element.183), channel_id=1, source_target_pairs={{0,16},{4,20},{8,24},{12,28},{16,0},{20,4},{24,8},{28,12},{1,17},{... | collective-permute-start | bytes 589832 | tf_op jit(solution)/shard_map/cond/branch_1_fun/ppermute | solution.py:294
  40.8 9.7 %outer.5 = (f32[3,16,1024]{2,1,0:T(8,128)S(1)}, f32[3,16,1024]{2,1,0:T(8,128)S(1)}, f32[3,16,1024]{2,1,0:T(8,128)S(1)}, f32[3,16,1024]{2,1,0:T(8,128)S(1)}, f32[16,4096]{1,0:T(8,128)S(1)}) custom-call(s32[5]{0:T(128)S(1)} %get-tuple-element.78.at_ref, f32[1,3,32,4096]{3,2,1,0:T(8,128)} %get-tuple-element.82.fields_ref, f32[32,4096]{1,0:T(8,128)S(1)} %copy-done.1, ...), custom_call_target="tpu_custom_call" | custom-call | tf_op jit(solution)/shard_map/cond/branch_1_fun/outer/pallas_call | solution.py:120
  50.4 1.7 %collective-permute-start.26 = (f32[3,16,1024]{2,1,0:T(8,128)S(1)}, f32[3,16,1024]{2,1,0:T(8,128)S(1)}, u32[]{:S(2)}, u32[]{:S(2)}) collective-permute-start(f32[3,16,1024]{2,1,0:T(8,128)S(1)} %get-tuple-element.95), channel_id=1, source_target_pairs={{0,4},{4,0},{8,12},{12,8},{16,20},{20,16},{24,28},{28,24},{1,5},{5... | collective-permute-start | bytes 589832 | tf_op jit(solution)/shard_map/cond/branch_1_fun/ppermute | solution.py:294
  52.2 1.6 %collective-permute-start.27 = (f32[3,16,1024]{2,1,0:T(8,128)S(1)}, f32[3,16,1024]{2,1,0:T(8,128)S(1)}, u32[]{:S(2)}, u32[]{:S(2)}) collective-permute-start(f32[3,16,1024]{2,1,0:T(8,128)S(1)} %get-tuple-element.96), channel_id=1, source_target_pairs={{0,8},{4,12},{8,0},{12,4},{16,24},{20,28},{24,16},{28,20},{1,9},{5... | collective-permute-start | bytes 589832 | tf_op jit(solution)/shard_map/cond/branch_1_fun/ppermute | solution.py:294
  55.2 2.7 %collective-permute-start.43 = (f32[3,16,1024]{2,1,0:T(8,128)S(1)}, f32[3,16,1024]{2,1,0:T(8,128)S(1)}, u32[]{:S(2)}, u32[]{:S(2)}) collective-permute-start(f32[3,16,1024]{2,1,0:T(8,128)S(1)} %get-tuple-element.173), channel_id=1, source_target_pairs={{0,12},{4,8},{8,4},{12,0},{16,28},{20,24},{24,20},{28,16},{1,13},{... | collective-permute-start | bytes 589832 | tf_op jit(solution)/shard_map/cond/branch_1_fun/ppermute | solution.py:294
  59.9 4.2 %collective-permute-done.28 = f32[3,16,1024]{2,1,0:T(8,128)S(1)} collective-permute-done((f32[3,16,1024]{2,1,0:T(8,128)S(1)}, f32[3,16,1024]{2,1,0:T(8,128)S(1)}, u32[]{:S(2)}, u32[]{:S(2)}) %collective-permute-start.28) | collective-permute-done | bytes 196640 | tf_op jit(solution)/shard_map/cond/branch_1_fun/ppermute | solution.py:294
  64.1 2.7 %collective-permute-start.35 = (f32[3,16,1024]{2,1,0:T(8,128)S(1)}, f32[3,16,1024]{2,1,0:T(8,128)S(1)}, u32[]{:S(2)}, u32[]{:S(2)}) collective-permute-start(f32[3,16,1024]{2,1,0:T(8,128)S(1)} %get-tuple-element.181), channel_id=1, source_target_pairs={{0,16},{4,20},{8,24},{12,28},{16,0},{20,4},{24,8},{28,12},{1,17},{... | collective-permute-start | bytes 589832 | tf_op jit(solution)/shard_map/cond/branch_1_fun/ppermute | solution.py:294
  67.1 5.6 %misfit.5 = f32[8,128]{1,0:T(8,128)S(1)} custom-call(s32[5]{0:T(128)S(1)} %get-tuple-element.78.at_ref, s32[256]{0:T(256)S(1)} %copy-done.11, f32[256]{0:T(256)S(1)} %copy-done.15, f32[256]{0:T(256)S(1)} %copy-done.19, f32[16,4096]{1,0:T(8,128)S(1)} %get-tuple-element.84.inner_ref, f32[16,4096]{1,0:T(8,128)S(1)} %get-tuple-element.98.outer_ref), custom_call_target="tpu_custom_call" | custom-call | tf_op jit(solution)/shard_map/cond/branch_1_fun/misfit/pallas_call | solution.py:174
  74.9 4.4 %collective-permute-done.42.refs_2_ = f32[3,16,1024]{2,1,0:T(8,128)S(1)} collective-permute-done((f32[3,16,1024]{2,1,0:T(8,128)S(1)}, f32[3,16,1024]{2,1,0:T(8,128)S(1)}, u32[]{:S(2)}, u32[]{:S(2)}) %collective-permute-start.42) | collective-permute-done | bytes 196640 | tf_op jit(solution)/shard_map/cond/branch_1_fun/ppermute | solution.py:294
  79.3 1.4 %place.10.refs_4_ = f32[1,3,32,4096]{3,2,1,0:T(8,128)} custom-call(s32[5]{0:T(128)S(1)} %get-tuple-element.78.at_ref, f32[3,16,1024]{2,1,0:T(8,128)S(1)} %get-tuple-element.176.refs_0_, f32[3,16,1024]{2,1,0:T(8,128)S(1)} %collective-permute-done.41.refs_1_, f32[3,16,1024]{2,1,0:T(8,128)S(1)} %collective-permute-done.42.refs_2_, ...), custom_call_target="tpu_custom_call" | custom-call | tf_op jit(solution)/shard_map/cond/branch_1_fun/place/pallas_call | solution.py:228
  81.4 4.2 %collective-permute-start.30 = (f32[]{:T(128)}, f32[]{:T(128)}, u32[]{:S(2)}, u32[]{:S(2)}) collective-permute-start(f32[]{:T(128)} %add.60), channel_id=1, source_target_pairs={{0,2},{1,3},{2,0},{3,1},{4,6},{5,7},{6,4},{7,5},{8,10},{9,11},{10,... | collective-permute-start | bytes 20 | tf_op jit(solution)/shard_map/cond/branch_1_fun/ppermute | solution.py:189
  86.5 1.7 %collective-permute-start.31 = (f32[8]{0:T(128)S(1)}, f32[8]{0:T(128)S(1)}, u32[]{:S(2)}, u32[]{:S(2)}) collective-permute-start(f32[8]{0:T(128)S(1)} %compare_select_fusion.1), channel_id=1, source_target_pairs={{0,4},{4,0},{8,12},{12,8},{16,20},{20,16},{24,28},{28,24},{1,5},{5... | collective-permute-start | bytes 104 | tf_op jit(solution)/shard_map/cond/branch_1_fun/ppermute | solution.py:189
  88.3 1.9 %collective-permute-done.31 = f32[8]{0:T(128)S(1)} collective-permute-done((f32[8]{0:T(128)S(1)}, f32[8]{0:T(128)S(1)}, u32[]{:S(2)}, u32[]{:S(2)}) %collective-permute-start.31) | collective-permute-done | bytes 64 | tf_op jit(solution)/shard_map/cond/branch_1_fun/ppermute | solution.py:189
  90.2 1.5 %collective-permute-start.32 = (f32[8]{0:T(128)S(1)}, f32[8]{0:T(128)S(1)}, u32[]{:S(2)}, u32[]{:S(2)}) collective-permute-start(f32[8]{0:T(128)S(1)} %fusion.9), channel_id=1, source_target_pairs={{0,8},{4,12},{8,0},{12,4},{16,24},{20,28},{24,16},{28,20},{1,9},{5... | collective-permute-start | bytes 104 | tf_op jit(solution)/shard_map/cond/branch_1_fun/ppermute | solution.py:189
  91.6 2.1 %collective-permute-done.32 = f32[8]{0:T(128)S(1)} collective-permute-done((f32[8]{0:T(128)S(1)}, f32[8]{0:T(128)S(1)}, u32[]{:S(2)}, u32[]{:S(2)}) %collective-permute-start.32) | collective-permute-done | bytes 64 | tf_op jit(solution)/shard_map/cond/branch_1_fun/ppermute | solution.py:189
  93.7 2.3 %collective-permute-start.33 = (f32[8]{0:T(128)S(1)}, f32[8]{0:T(128)S(1)}, u32[]{:S(2)}, u32[]{:S(2)}) collective-permute-start(f32[8]{0:T(128)S(1)} %fusion.13), channel_id=1, source_target_pairs={{0,16},{4,20},{8,24},{12,28},{16,0},{20,4},{24,8},{28,12},{1,17},{... | collective-permute-start | bytes 104 | tf_op jit(solution)/shard_map/cond/branch_1_fun/ppermute | solution.py:189
  96.1 1.6 %collective-permute-start.36 = (f32[3,16,1024]{2,1,0:T(8,128)S(1)}, f32[3,16,1024]{2,1,0:T(8,128)S(1)}, u32[]{:S(2)}, u32[]{:S(2)}) collective-permute-start(f32[3,16,1024]{2,1,0:T(8,128)S(1)} %get-tuple-element.179), channel_id=1, source_target_pairs={{0,4},{4,0},{8,12},{12,8},{16,20},{20,16},{24,28},{28,24},{1,5},{5... | collective-permute-start | bytes 589832 | tf_op jit(solution)/shard_map/cond/branch_1_fun/ppermute | solution.py:294
  97.8 2.0 %collective-permute-start.38 = (f32[3,16,1024]{2,1,0:T(8,128)S(1)}, f32[3,16,1024]{2,1,0:T(8,128)S(1)}, u32[]{:S(2)}, u32[]{:S(2)}) collective-permute-start(f32[3,16,1024]{2,1,0:T(8,128)S(1)} %get-tuple-element.177), channel_id=1, source_target_pairs={{0,12},{4,8},{8,4},{12,0},{16,28},{20,24},{24,20},{28,16},{1,13},{... | collective-permute-start | bytes 589832 | tf_op jit(solution)/shard_map/cond/branch_1_fun/ppermute | solution.py:294
  105.8 1.5 %place.11 = f32[1,3,32,4096]{3,2,1,0:T(8,128)} custom-call(s32[5]{0:T(128)S(1)} %get-tuple-element.78.at_ref, f32[3,16,1024]{2,1,0:T(8,128)S(1)} %get-tuple-element.180.refs_0_, f32[3,16,1024]{2,1,0:T(8,128)S(1)} %collective-permute-done.36.refs_1_, f32[3,16,1024]{2,1,0:T(8,128)S(1)} %collective-permute-done.37.refs_2_, ...), custom_call_target="tpu_custom_call", output_to_operand_aliasing={{}: (5, {})} | custom-call | tf_op jit(solution)/shard_map/cond/branch_1_fun/place/pallas_call | solution.py:228
  (55 shorter events, 16.9 us)
Async XLA Ops:
  2.2 38.6 %copy-start.1 = (f32[32,4096]{1,0:T(8,128)S(1)}, f32[32,4096]{1,0:T(8,128)}, u32[]{:S(2)}) copy-start(f32[32,4096]{1,0:T(8,128)} %get-tuple-element.83.depth_ref) | copy-start | bytes 1572868 | tf_op jit(solution)/shard_map/cond
  10.1 11.8 %collective-permute-start.23 = (f32[3,16,1024]{2,1,0:T(8,128)S(1)}, f32[3,16,1024]{2,1,0:T(8,128)S(1)}, u32[]{:S(2)}, u32[]{:S(2)}) collective-permute-start(f32[3,16,1024]{2,1,0:T(8,128)S(1)} %get-tuple-element.89), channel_id=1, source_target_pairs={{0,4},{4,0},{8,12},{12,8},{16,20},{20,16},{24,28},{28,24},{1,5},{5... | collective-permute-start | bytes 589832 | tf_op jit(solution)/shard_map/cond/branch_1_fun/ppermute | solution.py:294
  13.2 8.7 %collective-permute-start.24 = (f32[3,16,1024]{2,1,0:T(8,128)S(1)}, f32[3,16,1024]{2,1,0:T(8,128)S(1)}, u32[]{:S(2)}, u32[]{:S(2)}) collective-permute-start(f32[3,16,1024]{2,1,0:T(8,128)S(1)} %get-tuple-element.90), channel_id=1, source_target_pairs={{0,8},{4,12},{8,0},{12,4},{16,24},{20,28},{24,16},{28,20},{1,9},{5... | collective-permute-start | bytes 589832 | tf_op jit(solution)/shard_map/cond/branch_1_fun/ppermute | solution.py:294
  14.7 8.8 %collective-permute-start.25 = (f32[3,16,1024]{2,1,0:T(8,128)S(1)}, f32[3,16,1024]{2,1,0:T(8,128)S(1)}, u32[]{:S(2)}, u32[]{:S(2)}) collective-permute-start(f32[3,16,1024]{2,1,0:T(8,128)S(1)} %get-tuple-element.91), channel_id=1, source_target_pairs={{0,12},{4,8},{8,4},{12,0},{16,28},{20,24},{24,20},{28,16},{1,13},{... | collective-permute-start | bytes 589832 | tf_op jit(solution)/shard_map/cond/branch_1_fun/ppermute | solution.py:294
  14.7 26.0 %collective-permute-start.21 = (f32[4,8,4096]{2,1,0:T(8,128)S(1)}, f32[4,8,4096]{2,1,0:T(8,128)S(1)}, u32[]{:S(2)}, u32[]{:S(2)}) collective-permute-start(f32[4,8,4096]{2,1,0:T(8,128)S(1)} %get-tuple-element.85), channel_id=1, source_target_pairs={{0,1},{1,2},{2,3},{4,5},{5,6},{6,7},{8,9},{9,10},{10,11},{12,13},{... | collective-permute-start | bytes 1572872 | tf_op jit(solution)/shard_map/cond/branch_1_fun/ppermute | solution.py:320
  16.1 24.7 %collective-permute-start.22 = (f32[4,8,4096]{2,1,0:T(8,128)S(1)}, f32[4,8,4096]{2,1,0:T(8,128)S(1)}, u32[]{:S(2)}, u32[]{:S(2)}) collective-permute-start(f32[4,8,4096]{2,1,0:T(8,128)S(1)} %get-tuple-element.86), channel_id=1, source_target_pairs={{1,0},{2,1},{3,2},{5,4},{6,5},{7,6},{9,8},{10,9},{11,10},{13,12},{... | collective-permute-start | bytes 1572872 | tf_op jit(solution)/shard_map/cond/branch_1_fun/ppermute | solution.py:321
  25.0 29.0 %collective-permute-start.40 = (f32[3,16,1024]{2,1,0:T(8,128)}, f32[3,16,1024]{2,1,0:T(8,128)}, u32[]{:S(2)}, u32[]{:S(2)}) collective-permute-start(f32[3,16,1024]{2,1,0:T(8,128)} %get-tuple-element.183), channel_id=1, source_target_pairs={{0,16},{4,20},{8,24},{12,28},{16,0},{20,4},{24,8},{28,12},{1,17},{... | collective-permute-start | bytes 589832 | tf_op jit(solution)/shard_map/cond/branch_1_fun/ppermute | solution.py:294
  27.8 26.2 %collective-permute-start.39 = (f32[3,16,1024]{2,1,0:T(8,128)}, f32[3,16,1024]{2,1,0:T(8,128)}, u32[]{:S(2)}, u32[]{:S(2)}) collective-permute-start(f32[3,16,1024]{2,1,0:T(8,128)} %get-tuple-element.184), channel_id=1, source_target_pairs={{0,16},{4,20},{8,24},{12,28},{16,0},{20,4},{24,8},{28,12},{1,17},{... | collective-permute-start | bytes 589832 | tf_op jit(solution)/shard_map/cond/branch_1_fun/ppermute | solution.py:294
  50.4 9.0 %collective-permute-start.26 = (f32[3,16,1024]{2,1,0:T(8,128)S(1)}, f32[3,16,1024]{2,1,0:T(8,128)S(1)}, u32[]{:S(2)}, u32[]{:S(2)}) collective-permute-start(f32[3,16,1024]{2,1,0:T(8,128)S(1)} %get-tuple-element.95), channel_id=1, source_target_pairs={{0,4},{4,0},{8,12},{12,8},{16,20},{20,16},{24,28},{28,24},{1,5},{5... | collective-permute-start | bytes 589832 | tf_op jit(solution)/shard_map/cond/branch_1_fun/ppermute | solution.py:294
  52.2 7.7 %collective-permute-start.27 = (f32[3,16,1024]{2,1,0:T(8,128)S(1)}, f32[3,16,1024]{2,1,0:T(8,128)S(1)}, u32[]{:S(2)}, u32[]{:S(2)}) collective-permute-start(f32[3,16,1024]{2,1,0:T(8,128)S(1)} %get-tuple-element.96), channel_id=1, source_target_pairs={{0,8},{4,12},{8,0},{12,4},{16,24},{20,28},{24,16},{28,20},{1,9},{5... | collective-permute-start | bytes 589832 | tf_op jit(solution)/shard_map/cond/branch_1_fun/ppermute | solution.py:294
  53.8 10.3 %collective-permute-start.28 = (f32[3,16,1024]{2,1,0:T(8,128)S(1)}, f32[3,16,1024]{2,1,0:T(8,128)S(1)}, u32[]{:S(2)}, u32[]{:S(2)}) collective-permute-start(f32[3,16,1024]{2,1,0:T(8,128)S(1)} %get-tuple-element.97), channel_id=1, source_target_pairs={{0,12},{4,8},{8,4},{12,0},{16,28},{20,24},{24,20},{28,16},{1,13},{... | collective-permute-start | bytes 589832 | tf_op jit(solution)/shard_map/cond/branch_1_fun/ppermute | solution.py:294
  55.2 18.7 %collective-permute-start.43 = (f32[3,16,1024]{2,1,0:T(8,128)S(1)}, f32[3,16,1024]{2,1,0:T(8,128)S(1)}, u32[]{:S(2)}, u32[]{:S(2)}) collective-permute-start(f32[3,16,1024]{2,1,0:T(8,128)S(1)} %get-tuple-element.173), channel_id=1, source_target_pairs={{0,12},{4,8},{8,4},{12,0},{16,28},{20,24},{24,20},{28,16},{1,13},{... | collective-permute-start | bytes 589832 | tf_op jit(solution)/shard_map/cond/branch_1_fun/ppermute | solution.py:294
  57.9 21.4 %collective-permute-start.42 = (f32[3,16,1024]{2,1,0:T(8,128)S(1)}, f32[3,16,1024]{2,1,0:T(8,128)S(1)}, u32[]{:S(2)}, u32[]{:S(2)}) collective-permute-start(f32[3,16,1024]{2,1,0:T(8,128)S(1)} %get-tuple-element.174), channel_id=1, source_target_pairs={{0,8},{4,12},{8,0},{12,4},{16,24},{20,28},{24,16},{28,20},{1,9},{5... | collective-permute-start | bytes 589832 | tf_op jit(solution)/shard_map/cond/branch_1_fun/ppermute | solution.py:294
  59.5 19.9 %collective-permute-start.41 = (f32[3,16,1024]{2,1,0:T(8,128)S(1)}, f32[3,16,1024]{2,1,0:T(8,128)S(1)}, u32[]{:S(2)}, u32[]{:S(2)}) collective-permute-start(f32[3,16,1024]{2,1,0:T(8,128)S(1)} %get-tuple-element.175), channel_id=1, source_target_pairs={{0,4},{4,0},{8,12},{12,8},{16,20},{20,16},{24,28},{28,24},{1,5},{5... | collective-permute-start | bytes 589832 | tf_op jit(solution)/shard_map/cond/branch_1_fun/ppermute | solution.py:294
  64.1 31.9 %collective-permute-start.35 = (f32[3,16,1024]{2,1,0:T(8,128)S(1)}, f32[3,16,1024]{2,1,0:T(8,128)S(1)}, u32[]{:S(2)}, u32[]{:S(2)}) collective-permute-start(f32[3,16,1024]{2,1,0:T(8,128)S(1)} %get-tuple-element.181), channel_id=1, source_target_pairs={{0,16},{4,20},{8,24},{12,28},{16,0},{20,4},{24,8},{28,12},{1,17},{... | collective-permute-start | bytes 589832 | tf_op jit(solution)/shard_map/cond/branch_1_fun/ppermute | solution.py:294
  66.8 29.2 %collective-permute-start.34 = (f32[3,16,1024]{2,1,0:T(8,128)S(1)}, f32[3,16,1024]{2,1,0:T(8,128)S(1)}, u32[]{:S(2)}, u32[]{:S(2)}) collective-permute-start(f32[3,16,1024]{2,1,0:T(8,128)S(1)} %get-tuple-element.182), channel_id=1, source_target_pairs={{0,16},{4,20},{8,24},{12,28},{16,0},{20,4},{24,8},{28,12},{1,17},{... | collective-permute-start | bytes 589832 | tf_op jit(solution)/shard_map/cond/branch_1_fun/ppermute | solution.py:294
  73.9 6.9 %collective-permute-start.29 = (f32[]{:T(128)}, f32[]{:T(128)}, u32[]{:S(2)}, u32[]{:S(2)}) collective-permute-start(f32[]{:T(128)} %bitcast.27), channel_id=1, source_target_pairs={{0,1},{1,0},{2,3},{3,2},{4,5},{5,4},{6,7},{7,6},{8,9},{9,8},{10,11... | collective-permute-start | bytes 20 | tf_op jit(solution)/shard_map/cond/branch_1_fun/ppermute | solution.py:189
  81.4 4.5 %collective-permute-start.30 = (f32[]{:T(128)}, f32[]{:T(128)}, u32[]{:S(2)}, u32[]{:S(2)}) collective-permute-start(f32[]{:T(128)} %add.60), channel_id=1, source_target_pairs={{0,2},{1,3},{2,0},{3,1},{4,6},{5,7},{6,4},{7,5},{8,10},{9,11},{10,... | collective-permute-start | bytes 20 | tf_op jit(solution)/shard_map/cond/branch_1_fun/ppermute | solution.py:189
  86.5 3.6 %collective-permute-start.31 = (f32[8]{0:T(128)S(1)}, f32[8]{0:T(128)S(1)}, u32[]{:S(2)}, u32[]{:S(2)}) collective-permute-start(f32[8]{0:T(128)S(1)} %compare_select_fusion.1), channel_id=1, source_target_pairs={{0,4},{4,0},{8,12},{12,8},{16,20},{20,16},{24,28},{28,24},{1,5},{5... | collective-permute-start | bytes 104 | tf_op jit(solution)/shard_map/cond/branch_1_fun/ppermute | solution.py:189
  90.2 3.5 %collective-permute-start.32 = (f32[8]{0:T(128)S(1)}, f32[8]{0:T(128)S(1)}, u32[]{:S(2)}, u32[]{:S(2)}) collective-permute-start(f32[8]{0:T(128)S(1)} %fusion.9), channel_id=1, source_target_pairs={{0,8},{4,12},{8,0},{12,4},{16,24},{20,28},{24,16},{28,20},{1,9},{5... | collective-permute-start | bytes 104 | tf_op jit(solution)/shard_map/cond/branch_1_fun/ppermute | solution.py:189
  93.7 6.2 %collective-permute-start.33 = (f32[8]{0:T(128)S(1)}, f32[8]{0:T(128)S(1)}, u32[]{:S(2)}, u32[]{:S(2)}) collective-permute-start(f32[8]{0:T(128)S(1)} %fusion.13), channel_id=1, source_target_pairs={{0,16},{4,20},{8,24},{12,28},{16,0},{20,4},{24,8},{28,12},{1,17},{... | collective-permute-start | bytes 104 | tf_op jit(solution)/shard_map/cond/branch_1_fun/ppermute | solution.py:189
  96.1 7.3 %collective-permute-start.36 = (f32[3,16,1024]{2,1,0:T(8,128)S(1)}, f32[3,16,1024]{2,1,0:T(8,128)S(1)}, u32[]{:S(2)}, u32[]{:S(2)}) collective-permute-start(f32[3,16,1024]{2,1,0:T(8,128)S(1)} %get-tuple-element.179), channel_id=1, source_target_pairs={{0,4},{4,0},{8,12},{12,8},{16,20},{20,16},{24,28},{28,24},{1,5},{5... | collective-permute-start | bytes 589832 | tf_op jit(solution)/shard_map/cond/branch_1_fun/ppermute | solution.py:294
  97.8 6.8 %collective-permute-start.38 = (f32[3,16,1024]{2,1,0:T(8,128)S(1)}, f32[3,16,1024]{2,1,0:T(8,128)S(1)}, u32[]{:S(2)}, u32[]{:S(2)}) collective-permute-start(f32[3,16,1024]{2,1,0:T(8,128)S(1)} %get-tuple-element.177), channel_id=1, source_target_pairs={{0,12},{4,8},{8,4},{12,0},{16,28},{20,24},{24,20},{28,16},{1,13},{... | collective-permute-start | bytes 589832 | tf_op jit(solution)/shard_map/cond/branch_1_fun/ppermute | solution.py:294
  99.8 6.1 %collective-permute-start.37 = (f32[3,16,1024]{2,1,0:T(8,128)S(1)}, f32[3,16,1024]{2,1,0:T(8,128)S(1)}, u32[]{:S(2)}, u32[]{:S(2)}) collective-permute-start(f32[3,16,1024]{2,1,0:T(8,128)S(1)} %get-tuple-element.178), channel_id=1, source_target_pairs={{0,8},{4,12},{8,0},{12,4},{16,24},{20,28},{24,16},{28,20},{1,9},{5... | collective-permute-start | bytes 589832 | tf_op jit(solution)/shard_map/cond/branch_1_fun/ppermute | solution.py:294
  (5 other events, 49.9 us)
where the time goes:
time: 109 us
  starting transfers between devices  34.7 us (32%)
  Pallas kernels  27.5 us (25%)
  loops' own time  20.3 us (19%)
  waiting for transfers between devices  17.2 us (16%)
  other arithmetic  5.12 us (5%)
  local copies, waits for them, and re-layouts  1.98 us (2%)
  between operations  1.84 us (2%)
    ppermute x16, starting transfers between devices, to_mate(): lax.ppermute(x, 'dom', [(i, i ^ m) for i in range(lax.axis_size('dom'))])  21.4 us
    another operation x1, loops' own time, shards(): lax.switch(jnp.clip(routes[0] - 1, 0, half - 1), branches, routes, at, fi...  20.3 us
    pallas_call x2, Pallas kernels, forecast(): pl.pallas_call(kernel, out_shape=[jax.ShapeDtypeStruct(shape, jnp.float32...  17.6 us
    ppermute x16, waiting for transfers between devices, to_mate(): lax.ppermute(x, 'dom', [(i, i ^ m) for i in range(lax.axis_size('dom'))])  12.9 us
    ppermute x5, starting transfers between devices, sum_over(): x = x + lax.ppermute(x, axis, [(i, i ^ step) for i in range(count)])  10.7 us
    pallas_call x1, Pallas kernels, misfit(): pl.pallas_call(misfit_kernel, out_shape=jax.ShapeDtypeStruct((8, LANES),...  5.61 us
    ppermute x5, waiting for transfers between devices, sum_over(): x = x + lax.ppermute(x, axis, [(i, i ^ step) for i in range(count)])  4.29 us
    pallas_call x2, Pallas kernels, place(): pl.pallas_call(kernel, out_shape=pltpu.HBM(shape, jnp.float32), in_specs=...  2.93 us
  transfers between devices with their start and end apart: 23, of which 9 were waited for; matrix products, arithmetic and copies ran while one was open for 6% of the time, Pallas kernels for 15%

commit v1 on v0

--- a/solution.py
+++ b/solution.py
@@ -18,110 +18,81 @@
 in_hbm = pl.BlockSpec(memory_space=pltpu.HBM)
 
 
-def forecast_steps(h, u, v, d, top_open=None, bottom_open=None):
-    n_rows, n_cols = h.shape
-    for _ in range(STEPS):
-        du = d * u
-        dv = d * v
-        dx = 0.5 * (pltpu.roll(du, n_cols - 1, 1) - pltpu.roll(du, 1, 1))
-        dy = 0.5 * (pltpu.roll(dv, n_rows - 1, 0) - pltpu.roll(dv, 1, 0))
-        h = h - time_step * (dx + dy)
+def model_steps(h_ref, u_ref, v_ref, d_ref, top_open=None, bottom_open=None):
+    n_rows, n_cols = h_ref.shape
+    h_ref[...] = h_ref[...] * (0.5 * time_step)
+    d_ref[...] = d_ref[...] * (0.25 * time_step * time_step)
+
+    def cols(a):
+        return pltpu.roll(a, n_cols - 1, 1) - pltpu.roll(a, 1, 1)
+
+    def rows(a):
+        return pltpu.roll(a, n_rows - 1, 0) - pltpu.roll(a, 1, 0)
+
+    def step(_, carry):
+        u = u_ref[...]
+        v = v_ref[...]
+        d = d_ref[...]
+        h = h_ref[...] - (cols(d * u) + rows(d * v))
         if top_open is not None:
             h = jnp.concatenate(
                 [h[:HALO] * top_open, h[HALO : n_rows - HALO], h[n_rows - HALO :] * bottom_open], axis=0
             )
-        dx = 0.5 * (pltpu.roll(h, n_cols - 1, 1) - pltpu.roll(h, 1, 1))
-        u = u - time_step * dx + (time_step * coriolis) * v
-        dy = 0.5 * (pltpu.roll(h, n_rows - 1, 0) - pltpu.roll(h, 1, 0))
-        v = v - time_step * dy - (time_step * coriolis) * u
-    return h, u, v
-
-
-def chunk_width(n_cols, piece):
-    return min(512, piece)
-
-
-def window_columns(rows_of, start, width, n_cols, n_rows):
-    left = pl.multiple_of(lax.rem(start + n_cols - LANES, n_cols), LANES)
-    right = pl.multiple_of(lax.rem(start + width, n_cols), LANES)
-    lane = lax.broadcasted_iota(jnp.int32, (n_rows, LANES), 1)
-
-    def window(k):
-        rim = jnp.where(lane < LANES // 2, rows_of(k, right, LANES), rows_of(k, left, LANES))
-        return jnp.concatenate([rows_of(k, start, width), rim], axis=1)
-
-    return [window(k) for k in range(4)]
-
-
-def over_pieces(at_ref, n_cols, outs, work):
-    piece = n_cols // len(outs)
-    width = chunk_width(n_cols, piece)
-    parts = piece // width
-
-    def part(i, carry):
-        m = i // parts
-        inner = pl.multiple_of(i % parts * width, LANES)
-        start = pl.multiple_of(jnp.bitwise_xor(at_ref[0], m) * piece + inner, LANES)
-        done = work(start, width)
-        for to, out in enumerate(outs):
-
-            @pl.when(m == to)
-            def _(out=out):
-                for k in range(3):
-                    out[k, :, pl.ds(inner, width)] = done[k]
-
+        h_ref[...] = h
+        u = u - cols(h) + (time_step * coriolis) * v
+        u_ref[...] = u
+        v_ref[...] = v - rows(h) - (time_step * coriolis) * u
         return carry
 
-    lax.fori_loop(0, len(outs) * parts, part, 0)
+    lax.fori_loop(0, STEPS, step, 0)
+    h_ref[...] = h_ref[...] * (2.0 / time_step)
+
+
+def store_pieces(at_ref, outs, state, rows_of):
+    width = outs[0].shape[-1]
+    for m, out in enumerate(outs):
+        start = pl.multiple_of(jnp.bitwise_xor(at_ref[0], m) * width, LANES)
+        for k, ref in enumerate(state[:3]):
+            out[k] = rows_of(ref, pl.ds(start, width))
 
 
 def inner_kernel(at_ref, fields_ref, depth_ref, *refs):
-    outs, (h_ref, head_ref, tail_ref) = refs[:-3], refs[-3:]
-    n_rows, n_cols = depth_ref.shape
-
-    def rows_of(k, at, size):
-        return depth_ref[:, pl.ds(at, size)] if k == 3 else fields_ref[0, k, :, pl.ds(at, size)]
-
-    def work(start, width):
-        columns = window_columns(rows_of, start, width, n_cols, n_rows)
-        for k in range(4):
-            head_ref[k, :, pl.ds(start, width)] = columns[k][:HALO, :width]
-            tail_ref[k, :, pl.ds(start, width)] = columns[k][n_rows - HALO :, :width]
-        done = forecast_steps(*columns)
-        done = [x[HALO : n_rows - HALO, :width] for x in done]
-        h_ref[:, pl.ds(start, width)] = done[0]
-        return done
-
-    over_pieces(at_ref, n_cols, outs, work)
+    outs, (h_ref, head_ref, tail_ref), state = refs[:-7], refs[-7:-4], refs[-4:]
+    n_rows = depth_ref.shape[0]
+    for k in range(4):
+        field = depth_ref[...] if k == 3 else fields_ref[0, k]
+        state[k][...] = field
+        head_ref[k] = field[:HALO]
+        tail_ref[k] = field[n_rows - HALO :]
+    model_steps(*state)
+    h_ref[...] = state[0][HALO : n_rows - HALO]
+    store_pieces(at_ref, outs, state, lambda ref, at: ref[HALO : n_rows - HALO, at])
 
 
 def outer_kernel(at_ref, fields_ref, depth_ref, above_ref, below_ref, *refs):
-    outs, h_ref = refs[:-1], refs[-1]
-    n_rows, n_cols = depth_ref.shape
-    top_open = at_ref[1].astype(jnp.float32)
-    bottom_open = at_ref[2].astype(jnp.float32)
-
-    def rows_of(k, at, size):
-        mid = depth_ref[:, pl.ds(at, size)] if k == 3 else fields_ref[0, k, :, pl.ds(at, size)]
-        return jnp.concatenate([above_ref[k, :, pl.ds(at, size)], mid, below_ref[k, :, pl.ds(at, size)]], axis=0)
-
-    def work(start, width):
-        columns = window_columns(rows_of, start, width, n_cols, n_rows + 2 * HALO)
-        done = forecast_steps(*columns, top_open, bottom_open)
-        done = [jnp.concatenate([x[HALO : 2 * HALO, :width], x[n_rows : n_rows + HALO, :width]], axis=0) for x in done]
-        h_ref[:, pl.ds(start, width)] = done[0]
-        return done
-
-    over_pieces(at_ref, n_cols, outs, work)
-
-
-def forecast(kernel, name, at, arrays, n_rows, n_cols, count, extra=()):
+    outs, h_ref, state = refs[:-5], refs[-5], refs[-4:]
+    n_rows = depth_ref.shape[0]
+    for k in range(4):
+        state[k][:HALO] = above_ref[k]
+        state[k][HALO : HALO + n_rows] = depth_ref[...] if k == 3 else fields_ref[0, k]
+        state[k][HALO + n_rows :] = below_ref[k]
+    model_steps(*state, at_ref[1].astype(jnp.float32), at_ref[2].astype(jnp.float32))
+
+    def outer_rows(ref, at):
+        return jnp.concatenate([ref[HALO : 2 * HALO, at], ref[n_rows : n_rows + HALO, at]], axis=0)
+
+    h_ref[...] = outer_rows(state[0], pl.ds(0, depth_ref.shape[1]))
+    store_pieces(at_ref, outs, state, outer_rows)
+
+
+def forecast(kernel, name, at, arrays, n_rows, n_cols, count, window_rows, extra=()):
     shapes = [(3, n_rows, n_cols // count)] * count + [(n_rows, n_cols)] + list(extra)
     outs = pl.pallas_call(
         kernel,
         out_shape=[jax.ShapeDtypeStruct(shape, jnp.float32) for shape in shapes],
         in_specs=[in_smem] + [in_vmem] * len(arrays),
         out_specs=[in_vmem] * len(shapes),
+        scratch_shapes=[pltpu.VMEM((window_rows, n_cols), jnp.float32)] * 4,
         compiler_params=pltpu.CompilerParams(vmem_limit_bytes=VMEM_BYTES),
         name=name,
     )(at, *arrays)
@@ -298,8 +269,29 @@
     return [x if m == 0 else to_mate(x, m) for m, x in enumerate(pieces)]
 
 
+def pick(routes, first, sources, count):
+    def kernel(routes_ref, *refs):
+        srcs, outs = refs[: len(sources)], refs[len(sources) :]
+        for m, out in enumerate(outs):
+            which = routes_ref[first + m]
+            for s, src in enumerate(srcs):
+
+                @pl.when(which == s)
+                def _(src=src, out=out):
+                    out[...] = src[...]
+
+    return pl.pallas_call(
+        kernel,
+        out_shape=[jax.ShapeDtypeStruct(sources[0].shape, jnp.float32)] * count,
+        in_specs=[in_smem] + [in_vmem] * len(sources),
+        out_specs=[in_vmem] * count,
+        compiler_params=pltpu.CompilerParams(vmem_limit_bytes=VMEM_BYTES),
+        name="pick",
+    )(routes, *sources)
+
+
 def chosen(held, routes, crossing):
-    return [lax.select_n(routes[1 + k], *held) for k in range(crossing)]
+    return pick(routes, 1, held, crossing)
 
 
 def across(pieces, half):
@@ -307,8 +299,7 @@
 
 
 def for_slots(held, got, routes):
-    half = len(held)
-    return [lax.select_n(routes[1 + half + m], *held, *got) for m in range(half)]
+    return pick(routes, 1 + len(held), [*held, *got], len(held))
 
 
 def after(x, *earlier):
@@ -325,11 +316,13 @@
 def inner_forecast(at, fields, depth, count):
     n_rows, n_cols = depth.shape
     rim = (4, HALO, n_cols)
-    return forecast(inner_kernel, "inner", at, (fields, depth), n_rows - 2 * HALO, n_cols, count, (rim, rim))
+    return forecast(inner_kernel, "inner", at, (fields, depth), n_rows - 2 * HALO, n_cols, count, n_rows, (rim, rim))
 
 
 def outer_forecast(at, fields, depth, above, below, count):
-    return forecast(outer_kernel, "outer", at, (fields, depth, above, below), 2 * HALO, depth.shape[1], count)
+    n_rows, n_cols = depth.shape
+    arrays = (fields, depth, above, below)
+    return forecast(outer_kernel, "outer", at, arrays, 2 * HALO, n_cols, count, n_rows + 2 * HALO)
 
 
 def cycle(crossing, routes, at, fields, depth, obs_index, obs_value, obs_var):
@@ -344,7 +337,7 @@
     outer_held = among_mates(outer)
     outer_chosen = chosen(outer_held, routes, crossing)
     outer_got = across(outer_chosen, half)
-    log_weights = log_weight(misfit(at, obs_index, obs_value, obs_var, inner_h, after(outer_h, outer_chosen)))
+    log_weights = log_weight(after(misfit(at, obs_index, obs_value, obs_var, inner_h, outer_h), outer_chosen))
     inner_done = among_mates(for_slots(inner_held, after(inner_got, outer), routes))
     outer_done = among_mates(for_slots(outer_held, outer_got, routes))
     members = place(at, inner_done, ((0, HALO, n_rows - 2 * HALO),), fields.shape)

time: 109 us -> 93.8 us (0.86)
  loops' own time: 20.3 us -> 3.68 us
  waiting for transfers between devices: 17.2 us -> 30.3 us
  Pallas kernels: 27.5 us -> 23.1 us
  other arithmetic: 5.12 us -> 1.93 us
  starting transfers between devices: 34.7 us -> 32.1 us
  local copies, waits for them, and re-layouts: 1.98 us -> 0.62 us
    another operation x1, loops' own time: 20.3 us -> 3.68 us  [shards(): lax.switch(jnp.clip(routes[0] - 1, 0, half - 1), branches, routes, at, fi...]
    ppermute x16, waiting for transfers between devices: 12.9 us -> 22.9 us  [to_mate(): lax.ppermute(x, 'dom', [(i, i ^ m) for i in range(lax.axis_size('dom'))])]
    pallas_call x2, Pallas kernels: 17.6 us -> 10.7 us  [forecast(): pl.pallas_call(kernel, out_shape=[jax.ShapeDtypeStruct(shape, jnp.float32...]
    ppermute x5, starting transfers between devices: 10.7 us -> 6.18 us  [sum_over(): x = x + lax.ppermute(x, axis, [(i, i ^ step) for i in range(count)])]
    select_n x6 -> x0, other arithmetic: 3.25 us -> none  [the longest x4 2.38 us: for_slots(): lax.select_n(routes[1 + half + m], *held, *got)]
    ppermute x5, waiting for transfers between devices: 4.29 us -> 7.43 us  [sum_over(): x = x + lax.ppermute(x, axis, [(i, i ^ step) for i in range(count)])]
    pallas_call x0 -> x4, Pallas kernels: none -> 2.61 us  [pick(): pl.pallas_call(kernel, out_shape=[jax.ShapeDtypeStruct(sources[0].shape,...]
    ppermute x1, starting transfers between devices: 1.31 us -> 3.06 us  [halo_rows(): above = lax.ppermute(tail, 'rows', [(i, i + 1) for i in range(count - 1)])]
  transfers between devices with their start and end apart: 23 -> 23, of which waited for: 9 -> 11; matrix products, arithmetic and copies ran while one was open for 6% -> 3% of each run, Pallas kernels for 15% -> 16%
where the time goes in v1:
time: 93.8 us; the launch traced here: 93.6 us
  starting transfers between devices  32.1 us (34%)
  waiting for transfers between devices  30.3 us (32%)
  Pallas kernels  23.1 us (25%)
  loops' own time  3.68 us (4%)
  other arithmetic  1.93 us (2%)
  between operations  1.84 us (2%)
    ppermute x16, waiting for transfers between devices, to_mate(): lax.ppermute(x, 'dom', [(i, i ^ m) for i in range(lax.axis_size('dom'))])  22.9 us
    ppermute x16, starting transfers between devices, to_mate(): lax.ppermute(x, 'dom', [(i, i ^ m) for i in range(lax.axis_size('dom'))])  21.6 us
    pallas_call x2, Pallas kernels, forecast(): pl.pallas_call(kernel, out_shape=[jax.ShapeDtypeStruct(shape, jnp.float32...  10.7 us
    ppermute x5, waiting for transfers between devices, sum_over(): x = x + lax.ppermute(x, axis, [(i, i ^ step) for i in range(count)])  7.43 us
    ppermute x5, starting transfers between devices, sum_over(): x = x + lax.ppermute(x, axis, [(i, i ^ step) for i in range(count)])  6.18 us
    pallas_call x1, Pallas kernels, misfit(): pl.pallas_call(misfit_kernel, out_shape=jax.ShapeDtypeStruct((8, LANES),...  5.5 us
    another operation x1, loops' own time, shards(): lax.switch(jnp.clip(routes[0] - 1, 0, half - 1), branches, routes, at, fi...  3.68 us
    ppermute x1, starting transfers between devices, halo_rows(): above = lax.ppermute(tail, 'rows', [(i, i + 1) for i in range(count - 1)])  3.06 us
  transfers between devices with their start and end apart: 23, of which 11 were waited for; matrix products, arithmetic and copies ran while one was open for 3% of the time, Pallas kernels for 16%

profile of v1, /device:TPU:0, one launch (start us, length us, event | category | flops | bytes accessed | tf_op | source)
XLA Modules:
  0.0 93.6 jit_solution(1116623795432939549)
XLA Ops:
  2.1 90.3 %conditional.1 = (f32[1]{0:T(128)}, f32[1,3,32,4096]{3,2,1,0:T(8,128)}) conditional(s32[]{:T(128)} %bitcast.13, (s32[5]{0:T(128)S(1)}, f32[1,3,32,4096]{3,2,1,0:T(8,128)}, f32[32,4096]{1,0:T(8,128)}, s32[9]{0:T(128)S(1)}, s32[256]{0:T(256)}, /*index=5*/f32[256]{0:T(256)}, f32[256]{0:T(256)}) %tuple.35, ...), branch_computations={%region_0.3_spmd, %region_3.6_spmd, %region_6.9_spmd, %region_9.12... | conditional | flops 110 | bytes 28325956 | solution.py:360
  2.2 5.1 %inner.5 = (f32[3,16,1024]{2,1,0:T(8,128)S(1)}, f32[3,16,1024]{2,1,0:T(8,128)S(1)}, f32[3,16,1024]{2,1,0:T(8,128)S(1)}, f32[3,16,1024]{2,1,0:T(8,128)S(1)}, f32[...) custom-call(s32[5]{0:T(128)S(1)} %get-tuple-element.86.at_ref, ...), custom_call_target="tpu_custom_call" | custom-call | tf_op jit(solution)/shard_map/cond/branch_1_fun/inner/pallas_call | solution.py:90
  8.6 3.1 %collective-permute-start.21 = (f32[4,8,4096]{2,1,0:T(8,128)S(1)}, f32[4,8,4096]{2,1,0:T(8,128)S(1)}, u32[]{:S(2)}, u32[]{:S(2)}) collective-permute-start(f32[4,8,4096]{2,1,0:T(8,128)S(1)} %get-tuple-element.93), channel_id=1, source_target_pairs={{0,1},{1,2},{2,3},{4,5},{5,6},{6,7},{8,9},{9,10},{10,11},{12,13},{... | collective-permute-start | bytes 1572872 | tf_op jit(solution)/shard_map/cond/branch_1_fun/ppermute | solution.py:311
  11.6 3.0 %collective-permute-start.23 = (f32[3,16,1024]{2,1,0:T(8,128)S(1)}, f32[3,16,1024]{2,1,0:T(8,128)S(1)}, u32[]{:S(2)}, u32[]{:S(2)}) collective-permute-start(f32[3,16,1024]{2,1,0:T(8,128)S(1)} %get-tuple-element.97), channel_id=1, source_target_pairs={{0,4},{4,0},{8,12},{12,8},{16,20},{20,16},{24,28},{28,24},{1,5},{5... | collective-permute-start | bytes 589832 | tf_op jit(solution)/shard_map/cond/branch_1_fun/ppermute | solution.py:265
  14.7 1.6 %collective-permute-start.24 = (f32[3,16,1024]{2,1,0:T(8,128)S(1)}, f32[3,16,1024]{2,1,0:T(8,128)S(1)}, u32[]{:S(2)}, u32[]{:S(2)}) collective-permute-start(f32[3,16,1024]{2,1,0:T(8,128)S(1)} %get-tuple-element.98), channel_id=1, source_target_pairs={{0,8},{4,12},{8,0},{12,4},{16,24},{20,28},{24,16},{28,20},{1,9},{5... | collective-permute-start | bytes 589832 | tf_op jit(solution)/shard_map/cond/branch_1_fun/ppermute | solution.py:265
  16.3 3.6 %collective-permute-done.23.refs_1_ = f32[3,16,1024]{2,1,0:T(8,128)S(1)} collective-permute-done((f32[3,16,1024]{2,1,0:T(8,128)S(1)}, f32[3,16,1024]{2,1,0:T(8,128)S(1)}, u32[]{:S(2)}, u32[]{:S(2)}) %collective-permute-start.23) | collective-permute-done | bytes 196640 | tf_op jit(solution)/shard_map/cond/branch_1_fun/ppermute | solution.py:265
  19.9 2.6 %collective-permute-done.24.refs_2_ = f32[3,16,1024]{2,1,0:T(8,128)S(1)} collective-permute-done((f32[3,16,1024]{2,1,0:T(8,128)S(1)}, f32[3,16,1024]{2,1,0:T(8,128)S(1)}, u32[]{:S(2)}, u32[]{:S(2)}) %collective-permute-start.24) | collective-permute-done | bytes 196640 | tf_op jit(solution)/shard_map/cond/branch_1_fun/ppermute | solution.py:265
  22.5 3.5 %collective-permute-done.25.refs_3_ = f32[3,16,1024]{2,1,0:T(8,128)S(1)} collective-permute-done((f32[3,16,1024]{2,1,0:T(8,128)S(1)}, f32[3,16,1024]{2,1,0:T(8,128)S(1)}, u32[]{:S(2)}, u32[]{:S(2)}) %collective-permute-start.25) | collective-permute-done | bytes 196640 | tf_op jit(solution)/shard_map/cond/branch_1_fun/ppermute | solution.py:265
  26.5 3.2 %collective-permute-start.39 = (f32[3,16,1024]{2,1,0:T(8,128)S(1)}, f32[3,16,1024]{2,1,0:T(8,128)S(1)}, u32[]{:S(2)}, u32[]{:S(2)}) collective-permute-start(f32[3,16,1024]{2,1,0:T(8,128)S(1)} %get-tuple-element.100), channel_id=1, source_target_pairs={{0,16},{4,20},{8,24},{12,28},{16,0},{20,4},{24,8},{28,12},{1,17},{... | collective-permute-start | bytes 589832 | tf_op jit(solution)/shard_map/cond/branch_1_fun/ppermute | solution.py:265
  29.8 5.6 %outer.5 = (f32[3,16,1024]{2,1,0:T(8,128)S(1)}, f32[3,16,1024]{2,1,0:T(8,128)S(1)}, f32[3,16,1024]{2,1,0:T(8,128)S(1)}, f32[3,16,1024]{2,1,0:T(8,128)S(1)}, f32[16,4096]{1,0:T(8,128)S(1)}) custom-call(s32[5]{0:T(128)S(1)} %get-tuple-element.86.at_ref, f32[1,3,32,4096]{3,2,1,0:T(8,128)S(1)} %copy-done.1, f32[32,4096]{1,0:T(8,128)S(1)} %copy-done.5, ...), custom_call_target="tpu_custom_call" | custom-call | tf_op jit(solution)/shard_map/cond/branch_1_fun/outer/pallas_call | solution.py:90
  35.5 1.8 %collective-permute-start.26 = (f32[3,16,1024]{2,1,0:T(8,128)S(1)}, f32[3,16,1024]{2,1,0:T(8,128)S(1)}, u32[]{:S(2)}, u32[]{:S(2)}) collective-permute-start(f32[3,16,1024]{2,1,0:T(8,128)S(1)} %get-tuple-element.105), channel_id=1, source_target_pairs={{0,4},{4,0},{8,12},{12,8},{16,20},{20,16},{24,28},{28,24},{1,5},{5... | collective-permute-start | bytes 589832 | tf_op jit(solution)/shard_map/cond/branch_1_fun/ppermute | solution.py:265
  37.3 1.6 %collective-permute-start.27 = (f32[3,16,1024]{2,1,0:T(8,128)S(1)}, f32[3,16,1024]{2,1,0:T(8,128)S(1)}, u32[]{:S(2)}, u32[]{:S(2)}) collective-permute-start(f32[3,16,1024]{2,1,0:T(8,128)S(1)} %get-tuple-element.106), channel_id=1, source_target_pairs={{0,8},{4,12},{8,0},{12,4},{16,24},{20,28},{24,16},{28,20},{1,9},{5... | collective-permute-start | bytes 589832 | tf_op jit(solution)/shard_map/cond/branch_1_fun/ppermute | solution.py:265
  39.0 4.9 %collective-permute-done.39.refs_4_ = f32[3,16,1024]{2,1,0:T(8,128)S(1)} collective-permute-done((f32[3,16,1024]{2,1,0:T(8,128)S(1)}, f32[3,16,1024]{2,1,0:T(8,128)S(1)}, u32[]{:S(2)}, u32[]{:S(2)}) %collective-permute-start.39) | collective-permute-done | bytes 196640 | tf_op jit(solution)/shard_map/cond/branch_1_fun/ppermute | solution.py:265
  43.9 3.5 %collective-permute-done.40.refs_5_ = f32[3,16,1024]{2,1,0:T(8,128)S(1)} collective-permute-done((f32[3,16,1024]{2,1,0:T(8,128)S(1)}, f32[3,16,1024]{2,1,0:T(8,128)S(1)}, u32[]{:S(2)}, u32[]{:S(2)}) %collective-permute-start.40) | collective-permute-done | bytes 196640 | tf_op jit(solution)/shard_map/cond/branch_1_fun/ppermute | solution.py:265
  48.2 1.6 %collective-permute-start.41 = (f32[3,16,1024]{2,1,0:T(8,128)S(1)}, f32[3,16,1024]{2,1,0:T(8,128)S(1)}, u32[]{:S(2)}, u32[]{:S(2)}) collective-permute-start(f32[3,16,1024]{2,1,0:T(8,128)S(1)} %get-tuple-element.118), channel_id=1, source_target_pairs={{0,4},{4,0},{8,12},{12,8},{16,20},{20,16},{24,28},{28,24},{1,5},{5... | collective-permute-start | bytes 589832 | tf_op jit(solution)/shard_map/cond/branch_1_fun/ppermute | solution.py:265
  51.7 5.5 %misfit.5 = f32[8,128]{1,0:T(8,128)S(1)} custom-call(s32[5]{0:T(128)S(1)} %get-tuple-element.86.at_ref, s32[256]{0:T(256)S(1)} %copy-done.9, f32[256]{0:T(256)S(1)} %copy-done.13, f32[256]{0:T(256)S(1)} %copy-done.17, f32[16,4096]{1,0:T(8,128)S(1)} %get-tuple-element.92.inner_ref, f32[16,4096]{1,0:T(8,128)S(1)} %get-tuple-element.103.outer_ref), custom_call_target="tpu_custom_call" | custom-call | tf_op jit(solution)/shard_map/cond/branch_1_fun/misfit/pallas_call | solution.py:145
  58.4 2.2 %collective-permute-start.34 = (f32[3,16,1024]{2,1,0:T(8,128)S(1)}, f32[3,16,1024]{2,1,0:T(8,128)S(1)}, u32[]{:S(2)}, u32[]{:S(2)}) collective-permute-start(f32[3,16,1024]{2,1,0:T(8,128)S(1)} %get-tuple-element.108), channel_id=1, source_target_pairs={{0,16},{4,20},{8,24},{12,28},{16,0},{20,4},{24,8},{28,12},{1,17},{... | collective-permute-start | bytes 589832 | tf_op jit(solution)/shard_map/cond/branch_1_fun/ppermute | solution.py:265
  67.8 2.2 %collective-permute-done.30 = f32[]{:T(128)} collective-permute-done((f32[]{:T(128)}, f32[]{:T(128)}, u32[]{:S(2)}, u32[]{:S(2)}) %collective-permute-start.30) | collective-permute-done | bytes 36 | tf_op jit(solution)/shard_map/cond/branch_1_fun/ppermute | solution.py:160
  70.7 1.9 %collective-permute-start.31 = (f32[8]{0:T(128)S(1)}, f32[8]{0:T(128)S(1)}, u32[]{:S(2)}, u32[]{:S(2)}) collective-permute-start(f32[8]{0:T(128)S(1)} %compare_select_fusion.1), channel_id=1, source_target_pairs={{0,4},{4,0},{8,12},{12,8},{16,20},{20,16},{24,28},{28,24},{1,5},{5... | collective-permute-start | bytes 104 | tf_op jit(solution)/shard_map/cond/branch_1_fun/ppermute | solution.py:160
  72.6 1.7 %collective-permute-done.31 = f32[8]{0:T(128)S(1)} collective-permute-done((f32[8]{0:T(128)S(1)}, f32[8]{0:T(128)S(1)}, u32[]{:S(2)}, u32[]{:S(2)}) %collective-permute-start.31) | collective-permute-done | bytes 64 | tf_op jit(solution)/shard_map/cond/branch_1_fun/ppermute | solution.py:160
  74.3 3.5 %collective-permute-done.32 = f32[8]{0:T(128)S(1)} collective-permute-done((f32[8]{0:T(128)S(1)}, f32[8]{0:T(128)S(1)}, u32[]{:S(2)}, u32[]{:S(2)}) %collective-permute-start.32) | collective-permute-done | bytes 64 | tf_op jit(solution)/shard_map/cond/branch_1_fun/ppermute | solution.py:160
  77.8 2.0 %collective-permute-start.33 = (f32[8]{0:T(128)S(1)}, f32[8]{0:T(128)S(1)}, u32[]{:S(2)}, u32[]{:S(2)}) collective-permute-start(f32[8]{0:T(128)S(1)} %fusion.9), channel_id=1, source_target_pairs={{0,16},{4,20},{8,24},{12,28},{16,0},{20,4},{24,8},{28,12},{1,17},{... | collective-permute-start | bytes 104 | tf_op jit(solution)/shard_map/cond/branch_1_fun/ppermute | solution.py:160
  82.1 2.0 %collective-permute-start.37 = (f32[3,16,1024]{2,1,0:T(8,128)S(1)}, f32[3,16,1024]{2,1,0:T(8,128)S(1)}, u32[]{:S(2)}, u32[]{:S(2)}) collective-permute-start(f32[3,16,1024]{2,1,0:T(8,128)S(1)} %get-tuple-element.113), channel_id=1, source_target_pairs={{0,8},{4,12},{8,0},{12,4},{16,24},{20,28},{24,16},{28,20},{1,9},{5... | collective-permute-start | bytes 589832 | tf_op jit(solution)/shard_map/cond/branch_1_fun/ppermute | solution.py:265
  88.4 2.3 %collective-permute-done.38.refs_3_ = f32[3,16,1024]{2,1,0:T(8,128)S(1)} collective-permute-done((f32[3,16,1024]{2,1,0:T(8,128)S(1)}, f32[3,16,1024]{2,1,0:T(8,128)S(1)}, u32[]{:S(2)}, u32[]{:S(2)}) %collective-permute-start.38) | collective-permute-done | bytes 196640 | tf_op jit(solution)/shard_map/cond/branch_1_fun/ppermute | solution.py:265
  (50 shorter events, 20.0 us)
Async XLA Ops:
  2.2 27.7 %copy-start.1 = (f32[1,3,32,4096]{3,2,1,0:T(8,128)S(1)}, f32[1,3,32,4096]{3,2,1,0:T(8,128)}, u32[]{:S(2)}) copy-start(f32[1,3,32,4096]{3,2,1,0:T(8,128)} %get-tuple-element.90.fields_ref) | copy-start | bytes 4718596 | tf_op jit(solution)/shard_map/cond
  7.3 22.5 %collective-permute-start.22 = (f32[4,8,4096]{2,1,0:T(8,128)S(1)}, f32[4,8,4096]{2,1,0:T(8,128)S(1)}, u32[]{:S(2)}, u32[]{:S(2)}) collective-permute-start(f32[4,8,4096]{2,1,0:T(8,128)S(1)} %get-tuple-element.94), channel_id=1, source_target_pairs={{1,0},{2,1},{3,2},{5,4},{6,5},{7,6},{9,8},{10,9},{11,10},{13,12},{... | collective-permute-start | bytes 1572872 | tf_op jit(solution)/shard_map/cond/branch_1_fun/ppermute | solution.py:312
  8.6 21.3 %collective-permute-start.21 = (f32[4,8,4096]{2,1,0:T(8,128)S(1)}, f32[4,8,4096]{2,1,0:T(8,128)S(1)}, u32[]{:S(2)}, u32[]{:S(2)}) collective-permute-start(f32[4,8,4096]{2,1,0:T(8,128)S(1)} %get-tuple-element.93), channel_id=1, source_target_pairs={{0,1},{1,2},{2,3},{4,5},{5,6},{6,7},{8,9},{9,10},{10,11},{12,13},{... | collective-permute-start | bytes 1572872 | tf_op jit(solution)/shard_map/cond/branch_1_fun/ppermute | solution.py:311
  11.6 8.2 %collective-permute-start.23 = (f32[3,16,1024]{2,1,0:T(8,128)S(1)}, f32[3,16,1024]{2,1,0:T(8,128)S(1)}, u32[]{:S(2)}, u32[]{:S(2)}) collective-permute-start(f32[3,16,1024]{2,1,0:T(8,128)S(1)} %get-tuple-element.97), channel_id=1, source_target_pairs={{0,4},{4,0},{8,12},{12,8},{16,20},{20,16},{24,28},{28,24},{1,5},{5... | collective-permute-start | bytes 589832 | tf_op jit(solution)/shard_map/cond/branch_1_fun/ppermute | solution.py:265
  14.7 7.8 %collective-permute-start.24 = (f32[3,16,1024]{2,1,0:T(8,128)S(1)}, f32[3,16,1024]{2,1,0:T(8,128)S(1)}, u32[]{:S(2)}, u32[]{:S(2)}) collective-permute-start(f32[3,16,1024]{2,1,0:T(8,128)S(1)} %get-tuple-element.98), channel_id=1, source_target_pairs={{0,8},{4,12},{8,0},{12,4},{16,24},{20,28},{24,16},{28,20},{1,9},{5... | collective-permute-start | bytes 589832 | tf_op jit(solution)/shard_map/cond/branch_1_fun/ppermute | solution.py:265
  16.3 9.7 %collective-permute-start.25 = (f32[3,16,1024]{2,1,0:T(8,128)S(1)}, f32[3,16,1024]{2,1,0:T(8,128)S(1)}, u32[]{:S(2)}, u32[]{:S(2)}) collective-permute-start(f32[3,16,1024]{2,1,0:T(8,128)S(1)} %get-tuple-element.99), channel_id=1, source_target_pairs={{0,12},{4,8},{8,4},{12,0},{16,28},{20,24},{24,20},{28,16},{1,13},{... | collective-permute-start | bytes 589832 | tf_op jit(solution)/shard_map/cond/branch_1_fun/ppermute | solution.py:265
  26.5 17.4 %collective-permute-start.39 = (f32[3,16,1024]{2,1,0:T(8,128)S(1)}, f32[3,16,1024]{2,1,0:T(8,128)S(1)}, u32[]{:S(2)}, u32[]{:S(2)}) collective-permute-start(f32[3,16,1024]{2,1,0:T(8,128)S(1)} %get-tuple-element.100), channel_id=1, source_target_pairs={{0,16},{4,20},{8,24},{12,28},{16,0},{20,4},{24,8},{28,12},{1,17},{... | collective-permute-start | bytes 589832 | tf_op jit(solution)/shard_map/cond/branch_1_fun/ppermute | solution.py:265
  29.7 17.8 %collective-permute-start.40 = (f32[3,16,1024]{2,1,0:T(8,128)S(1)}, f32[3,16,1024]{2,1,0:T(8,128)S(1)}, u32[]{:S(2)}, u32[]{:S(2)}) collective-permute-start(f32[3,16,1024]{2,1,0:T(8,128)S(1)} %get-tuple-element.101), channel_id=1, source_target_pairs={{0,16},{4,20},{8,24},{12,28},{16,0},{20,4},{24,8},{28,12},{1,17},{... | collective-permute-start | bytes 589832 | tf_op jit(solution)/shard_map/cond/branch_1_fun/ppermute | solution.py:265
  35.5 14.9 %collective-permute-start.26 = (f32[3,16,1024]{2,1,0:T(8,128)S(1)}, f32[3,16,1024]{2,1,0:T(8,128)S(1)}, u32[]{:S(2)}, u32[]{:S(2)}) collective-permute-start(f32[3,16,1024]{2,1,0:T(8,128)S(1)} %get-tuple-element.105), channel_id=1, source_target_pairs={{0,4},{4,0},{8,12},{12,8},{16,20},{20,16},{24,28},{28,24},{1,5},{5... | collective-permute-start | bytes 589832 | tf_op jit(solution)/shard_map/cond/branch_1_fun/ppermute | solution.py:265
  37.3 20.5 %collective-permute-start.27 = (f32[3,16,1024]{2,1,0:T(8,128)S(1)}, f32[3,16,1024]{2,1,0:T(8,128)S(1)}, u32[]{:S(2)}, u32[]{:S(2)}) collective-permute-start(f32[3,16,1024]{2,1,0:T(8,128)S(1)} %get-tuple-element.106), channel_id=1, source_target_pairs={{0,8},{4,12},{8,0},{12,4},{16,24},{20,28},{24,16},{28,20},{1,9},{5... | collective-permute-start | bytes 589832 | tf_op jit(solution)/shard_map/cond/branch_1_fun/ppermute | solution.py:265
  38.9 18.9 %collective-permute-start.28 = (f32[3,16,1024]{2,1,0:T(8,128)S(1)}, f32[3,16,1024]{2,1,0:T(8,128)S(1)}, u32[]{:S(2)}, u32[]{:S(2)}) collective-permute-start(f32[3,16,1024]{2,1,0:T(8,128)S(1)} %get-tuple-element.107), channel_id=1, source_target_pairs={{0,12},{4,8},{8,4},{12,0},{16,28},{20,24},{24,20},{28,16},{1,13},{... | collective-permute-start | bytes 589832 | tf_op jit(solution)/shard_map/cond/branch_1_fun/ppermute | solution.py:265
  48.2 13.8 %collective-permute-start.41 = (f32[3,16,1024]{2,1,0:T(8,128)S(1)}, f32[3,16,1024]{2,1,0:T(8,128)S(1)}, u32[]{:S(2)}, u32[]{:S(2)}) collective-permute-start(f32[3,16,1024]{2,1,0:T(8,128)S(1)} %get-tuple-element.118), channel_id=1, source_target_pairs={{0,4},{4,0},{8,12},{12,8},{16,20},{20,16},{24,28},{28,24},{1,5},{5... | collective-permute-start | bytes 589832 | tf_op jit(solution)/shard_map/cond/branch_1_fun/ppermute | solution.py:265
  49.8 13.1 %collective-permute-start.42 = (f32[3,16,1024]{2,1,0:T(8,128)S(1)}, f32[3,16,1024]{2,1,0:T(8,128)S(1)}, u32[]{:S(2)}, u32[]{:S(2)}) collective-permute-start(f32[3,16,1024]{2,1,0:T(8,128)S(1)} %get-tuple-element.119), channel_id=1, source_target_pairs={{0,8},{4,12},{8,0},{12,4},{16,24},{20,28},{24,16},{28,20},{1,9},{5... | collective-permute-start | bytes 589832 | tf_op jit(solution)/shard_map/cond/branch_1_fun/ppermute | solution.py:265
  50.4 14.0 %collective-permute-start.43 = (f32[3,16,1024]{2,1,0:T(8,128)S(1)}, f32[3,16,1024]{2,1,0:T(8,128)S(1)}, u32[]{:S(2)}, u32[]{:S(2)}) collective-permute-start(f32[3,16,1024]{2,1,0:T(8,128)S(1)} %get-tuple-element.120), channel_id=1, source_target_pairs={{0,12},{4,8},{8,4},{12,0},{16,28},{20,24},{24,20},{28,16},{1,13},{... | collective-permute-start | bytes 589832 | tf_op jit(solution)/shard_map/cond/branch_1_fun/ppermute | solution.py:265
  58.4 21.5 %collective-permute-start.34 = (f32[3,16,1024]{2,1,0:T(8,128)S(1)}, f32[3,16,1024]{2,1,0:T(8,128)S(1)}, u32[]{:S(2)}, u32[]{:S(2)}) collective-permute-start(f32[3,16,1024]{2,1,0:T(8,128)S(1)} %get-tuple-element.108), channel_id=1, source_target_pairs={{0,16},{4,20},{8,24},{12,28},{16,0},{20,4},{24,8},{28,12},{1,17},{... | collective-permute-start | bytes 589832 | tf_op jit(solution)/shard_map/cond/branch_1_fun/ppermute | solution.py:265
  60.6 19.2 %collective-permute-start.35 = (f32[3,16,1024]{2,1,0:T(8,128)S(1)}, f32[3,16,1024]{2,1,0:T(8,128)S(1)}, u32[]{:S(2)}, u32[]{:S(2)}) collective-permute-start(f32[3,16,1024]{2,1,0:T(8,128)S(1)} %get-tuple-element.109), channel_id=1, source_target_pairs={{0,16},{4,20},{8,24},{12,28},{16,0},{20,4},{24,8},{28,12},{1,17},{... | collective-permute-start | bytes 589832 | tf_op jit(solution)/shard_map/cond/branch_1_fun/ppermute | solution.py:265
  62.0 3.8 %collective-permute-start.29 = (f32[]{:T(128)}, f32[]{:T(128)}, u32[]{:S(2)}, u32[]{:S(2)}) collective-permute-start(f32[]{:T(128)} %mul.9), channel_id=1, source_target_pairs={{0,1},{1,0},{2,3},{3,2},{4,5},{5,4},{6,7},{7,6},{8,9},{9,8},{10,11... | collective-permute-start | bytes 20 | tf_op jit(solution)/shard_map/cond/branch_1_fun/ppermute | solution.py:160
  66.5 3.6 %collective-permute-start.30 = (f32[]{:T(128)}, f32[]{:T(128)}, u32[]{:S(2)}, u32[]{:S(2)}) collective-permute-start(f32[]{:T(128)} %add.60), channel_id=1, source_target_pairs={{0,2},{1,3},{2,0},{3,1},{4,6},{5,7},{6,4},{7,5},{8,10},{9,11},{10,... | collective-permute-start | bytes 20 | tf_op jit(solution)/shard_map/cond/branch_1_fun/ppermute | solution.py:160
  70.7 3.6 %collective-permute-start.31 = (f32[8]{0:T(128)S(1)}, f32[8]{0:T(128)S(1)}, u32[]{:S(2)}, u32[]{:S(2)}) collective-permute-start(f32[8]{0:T(128)S(1)} %compare_select_fusion.1), channel_id=1, source_target_pairs={{0,4},{4,0},{8,12},{12,8},{16,20},{20,16},{24,28},{28,24},{1,5},{5... | collective-permute-start | bytes 104 | tf_op jit(solution)/shard_map/cond/branch_1_fun/ppermute | solution.py:160
  74.3 3.5 %collective-permute-start.32 = (f32[8]{0:T(128)S(1)}, f32[8]{0:T(128)S(1)}, u32[]{:S(2)}, u32[]{:S(2)}) collective-permute-start(f32[8]{0:T(128)S(1)} %fusion.5), channel_id=1, source_target_pairs={{0,8},{4,12},{8,0},{12,4},{16,24},{20,28},{24,16},{28,20},{1,9},{5... | collective-permute-start | bytes 104 | tf_op jit(solution)/shard_map/cond/branch_1_fun/ppermute | solution.py:160
  77.8 6.3 %collective-permute-start.33 = (f32[8]{0:T(128)S(1)}, f32[8]{0:T(128)S(1)}, u32[]{:S(2)}, u32[]{:S(2)}) collective-permute-start(f32[8]{0:T(128)S(1)} %fusion.9), channel_id=1, source_target_pairs={{0,16},{4,20},{8,24},{12,28},{16,0},{20,4},{24,8},{28,12},{1,17},{... | collective-permute-start | bytes 104 | tf_op jit(solution)/shard_map/cond/branch_1_fun/ppermute | solution.py:160
  80.6 7.8 %collective-permute-start.36 = (f32[3,16,1024]{2,1,0:T(8,128)S(1)}, f32[3,16,1024]{2,1,0:T(8,128)S(1)}, u32[]{:S(2)}, u32[]{:S(2)}) collective-permute-start(f32[3,16,1024]{2,1,0:T(8,128)S(1)} %get-tuple-element.112), channel_id=1, source_target_pairs={{0,4},{4,0},{8,12},{12,8},{16,20},{20,16},{24,28},{28,24},{1,5},{5... | collective-permute-start | bytes 589832 | tf_op jit(solution)/shard_map/cond/branch_1_fun/ppermute | solution.py:265
  82.1 6.3 %collective-permute-start.37 = (f32[3,16,1024]{2,1,0:T(8,128)S(1)}, f32[3,16,1024]{2,1,0:T(8,128)S(1)}, u32[]{:S(2)}, u32[]{:S(2)}) collective-permute-start(f32[3,16,1024]{2,1,0:T(8,128)S(1)} %get-tuple-element.113), channel_id=1, source_target_pairs={{0,8},{4,12},{8,0},{12,4},{16,24},{20,28},{24,16},{28,20},{1,9},{5... | collective-permute-start | bytes 589832 | tf_op jit(solution)/shard_map/cond/branch_1_fun/ppermute | solution.py:265
  84.2 6.6 %collective-permute-start.38 = (f32[3,16,1024]{2,1,0:T(8,128)S(1)}, f32[3,16,1024]{2,1,0:T(8,128)S(1)}, u32[]{:S(2)}, u32[]{:S(2)}) collective-permute-start(f32[3,16,1024]{2,1,0:T(8,128)S(1)} %get-tuple-element.114), channel_id=1, source_target_pairs={{0,12},{4,8},{8,4},{12,0},{16,28},{20,24},{24,20},{28,16},{1,13},{... | collective-permute-start | bytes 589832 | tf_op jit(solution)/shard_map/cond/branch_1_fun/ppermute | solution.py:265
  (4 other events, 93.8 us)
